TPU v7x, 32 devices: a whole 2x2x4 slice. The times are simulated.
32 devices in a mesh: dp: 2 (over x), row: 4 (over z), col: 4 (over y, core).
Axes of the slice: x: 2, y: 2, z: 4, core: 2. Of those that a mesh axis runs over, the one named last changes fastest.
Arguments:
- tokens: bfloat16 [4, 2048, 2048], P('dp', 'row', 'col'), may hold values from -6 to 6
- lengths: int32 [4], P('dp'), may hold values from 682 to 2048, as said below
- cotangent: bfloat16 [4, 2048, 2048], P('dp', 'row', 'col'), may hold values from -6 to 6
- norm1_gain: float32 [2048], P('col'), may hold values from 0.25 to 1.75
- norm1_bias: float32 [2048], P('col'), may hold values from -3 to 3
- query_weight: bfloat16 [2048, 2048], P('col', 'row'), may hold values from -0.125 to 0.125
- kv_weight: bfloat16 [2048, 256], P('col'), may hold values from -0.125 to 0.125
- out_weight: bfloat16 [2048, 2048], P('row', 'col'), may hold values from -1 to 1
- norm2_gain: float32 [2048], P('col'), may hold values from 0.25 to 1.75
- norm2_bias: float32 [2048], P('col'), may hold values from -3 to 3
- up_weight: bfloat16 [2048, 8192], P('col', 'row'), may hold values from -0.125 to 0.125
- down_weight: bfloat16 [8192, 2048], P('row', 'col'), may hold values from -0.0625 to 0.0625
Outputs:
- out: bfloat16 [4, 2048, 2048], P('dp', 'row', 'col')
- grad_input: bfloat16 [4, 2048, 2048], P('dp', 'row', 'col')
- grad_norm1_gain: float32 [2048], P('col')
- grad_norm1_bias: float32 [2048], P('col')
- grad_query_weight: float32 [2048, 2048], P('col', 'row')
- grad_kv_weight: float32 [2048, 256], P('col')
- grad_out_weight: float32 [2048, 2048], P('row', 'col')
- grad_norm2_gain: float32 [2048], P('col')
- grad_norm2_bias: float32 [2048], P('col')
- grad_up_weight: float32 [2048, 8192], P('col', 'row')
- grad_down_weight: float32 [8192, 2048], P('row', 'col')
Inputs may be any that keep to these rules, and one draw needn't show every extreme that they name: `lengths`: entry s is the number of valid slots of sequence s; sequences s * 2 to s * 2 + 1 belong to index s of dp. Some sequence has all 2048 slots valid.
All inputs are finite; a program needn't handle non-finite values.
Results may differ from a plain program's by a relative error of at most 0.02.
Values may be sent and summed in bfloat16 or wider, within the bound.
A program may use at most 256 MiB of HBM per device.

v0:
```python
import jax
import jax.numpy as jnp
from jax import lax
from jax.sharding import PartitionSpec as P

eps = 1e-05
BF = jnp.bfloat16
F32 = jnp.float32


def mm(a, b, ca, cb):
    return lax.dot_general(a, b, (((ca,), (cb,)), ((), ())), preferred_element_type=F32)


def norm_stats(hidden):
    centre = jnp.mean(hidden, axis=1, keepdims=True)
    spread = jnp.mean(hidden * hidden, axis=1, keepdims=True) - centre * centre
    return (centre, lax.rsqrt(spread + eps))


def norm_apply(hidden, centre, inverse, gain, bias, keep):
    return (keep * ((hidden - centre) * inverse * gain + bias)).astype(BF)


def norm_backward(gradient, normed, inverse, gain, keep):
    masked = keep * gradient
    scaled = masked * gain
    first = jnp.mean(scaled, axis=1, keepdims=True)
    second = jnp.mean(scaled * normed, axis=1, keepdims=True)
    result = inverse * (scaled - first - normed * second)
    return (result, jnp.sum(masked * normed, axis=0), jnp.sum(masked, axis=0))


def turn(weight):
    return lax.all_to_all(weight, "col", 0, 1, tiled=True)


def turn_back(rows):
    return lax.all_to_all(rows, "col", 1, 0, tiled=True)


def gather(x, axes, dim=0):
    return lax.all_gather(x, axes, axis=dim, tiled=True)


def scatter(x, axes):
    return lax.psum_scatter(x, axes, scatter_dimension=0, tiled=True)


def pairs_allowed(first, count, keys, length):
    q = first + jnp.arange(count, dtype=jnp.int32)[:, None]
    k = jnp.arange(keys, dtype=jnp.int32)[None, :]
    return (k <= q) & (k < length)


def attend(queries, kv, lengths, first):
    b, t, width = queries.shape
    hd = kv.shape[2] // 2
    outs, logs = ([], [])
    for s in range(b):
        keys, values = (kv[s, :, :hd], kv[s, :, hd:])
        allowed = pairs_allowed(first, t, kv.shape[1], lengths[s])
        for h in range(width // hd):
            q = queries[s, :, h * hd : (h + 1) * hd]
            scores = jnp.where(allowed, mm(q, keys, 1, 1) * hd ** (-0.5), -jnp.inf)
            top = jnp.max(scores, axis=1, keepdims=True)
            log_total = top + jnp.log(jnp.sum(jnp.exp(scores - top), axis=1, keepdims=True))
            weights = jnp.exp(scores - log_total).astype(BF)
            outs.append(mm(weights, values, 1, 0).astype(BF))
            logs.append(log_total)
    n = width // hd
    out = jnp.stack([jnp.concatenate(outs[s * n : (s + 1) * n], axis=1) for s in range(b)])
    log = jnp.stack([jnp.concatenate(logs[s * n : (s + 1) * n], axis=1) for s in range(b)])
    return (out, log)


def attend_back(queries, kv, lengths, first, logs, grad):
    b, t, width = queries.shape
    hd = kv.shape[2] // 2
    scale = hd ** (-0.5)
    dqs, dkvs = ([], [])
    for s in range(b):
        keys, values = (kv[s, :, :hd], kv[s, :, hd:])
        allowed = pairs_allowed(first, t, kv.shape[1], lengths[s])
        dk = dv = 0.0
        dq = []
        for h in range(width // hd):
            q = queries[s, :, h * hd : (h + 1) * hd]
            g = grad[s, :, h * hd : (h + 1) * hd]
            scores = jnp.where(allowed, mm(q, keys, 1, 1) * scale, -jnp.inf)
            p = jnp.exp(scores - logs[s, :, h : h + 1])
            dp = mm(g, values, 1, 1)
            ds = (p * (dp - jnp.sum(p * dp, axis=1, keepdims=True))).astype(BF)
            dq.append((mm(ds, keys, 1, 0) * scale).astype(BF))
            dk = dk + mm(ds, q, 0, 0) * scale
            dv = dv + mm(p.astype(BF), g, 0, 0)
        dqs.append(jnp.concatenate(dq, axis=1))
        dkvs.append(jnp.concatenate([dk, dv], axis=1).astype(BF))
    return (jnp.stack(dqs), jnp.stack(dkvs))


def local(
    tokens,
    lengths,
    cotangent,
    norm1_gain,
    norm1_bias,
    query_weight,
    kv_weight,
    out_weight,
    norm2_gain,
    norm2_bias,
    up_weight,
    down_weight,
):
    b, t, f = tokens.shape
    nd, nr, nc = (lax.axis_size(a) for a in ("dp", "row", "col"))
    dp, row, col = (lax.axis_index(a) for a in ("dp", "row", "col"))
    m, d = (b * t, f * nc)
    own = m // nc
    hd = kv_weight.shape[1] // 2
    plane = ("dp", "col")
    slot = row * t + jnp.arange(t, dtype=jnp.int32)
    keep = (slot[None, :] < lengths[:, None]).astype(F32).reshape(m, 1)

    def mine(x):
        return lax.dynamic_slice_in_dim(x, col * own, own, 0)

    def half(w):
        n = w.shape[0] // nd
        return lax.dynamic_slice_in_dim(w, dp * n, n, 0)

    wq = gather(turn(query_weight.T), "row")
    wo = gather(turn(out_weight), "row")
    wu = gather(turn(half(up_weight.T)), "row")
    wd = gather(turn(half(down_weight)), "row")
    wkv = gather(kv_weight, "col")
    vectors = gather(jnp.stack([norm1_gain, norm1_bias, norm2_gain, norm2_bias]), "col", 1)
    gain1, bias1, gain2, bias2 = (vectors[i : i + 1] for i in range(4))
    x = gather(tokens.reshape(m, f), "col", 1)
    grad_final = (keep * cotangent.reshape(m, f).astype(F32)).astype(BF)
    grad_own = turn(grad_final)
    grad_all = gather(grad_own, plane)
    keep_own = mine(keep)
    centre, inverse = norm_stats(x.astype(F32))
    one = norm_apply(x.astype(F32), centre, inverse, gain1, bias1, keep)
    one_own = mine(one)
    queries = mm(one, wq, 1, 1).astype(BF).reshape(b, t, -1)
    kv_own = mm(one_own, wkv, 1, 0).astype(BF)
    kv = gather(kv_own, ("row", "col")).reshape(nr, b, t, 2 * hd)
    kv = kv.transpose(1, 0, 2, 3).reshape(b, nr * t, 2 * hd)
    attended, logs = attend(queries, kv, lengths, row * t)
    attended = attended.reshape(m, -1)
    x_own = mine(x).astype(F32)
    middle = x_own + scatter(mm(attended, wo, 1, 0).astype(BF), "col").astype(F32)
    centre2, inverse2 = norm_stats(middle)
    two_own = norm_apply(middle, centre2, inverse2, gain2, bias2, keep_own)
    two = gather(two_own, plane)
    sums = mm(two, wu, 1, 1)
    activated, pull = jax.vjp(lambda v: jax.nn.gelu(v, approximate=True), sums)
    activated = activated.astype(BF)
    ffn = scatter(mm(activated, wd, 1, 0).astype(BF), plane)
    out = turn_back((keep_own * (middle + ffn.astype(F32))).astype(BF))
    grad_act = mm(grad_all, wd, 1, 1)
    grad_up = pull(grad_act)[0].astype(BF)
    d_down = scatter(mm(activated, grad_all, 0, 0).astype(BF), "row")
    d_up = scatter(mm(grad_up, two, 0, 0).astype(BF), "row")
    e_two = scatter(mm(grad_up, wu, 1, 0).astype(BF), plane).astype(F32)
    normed2 = (middle - centre2) * inverse2
    back_two, g_gain2, g_bias2 = norm_backward(e_two, normed2, inverse2, gain2, keep_own)
    grad_middle = grad_own.astype(F32) + back_two
    grad_attn = gather(grad_middle.astype(BF), "col")
    grad_att = mm(grad_attn, wo, 1, 1).astype(BF)
    d_out = scatter(mm(attended, grad_attn, 0, 0).astype(BF), "row")
    dq, dkv = attend_back(queries, kv, lengths, row * t, logs, grad_att.reshape(b, t, -1))
    dq = dq.reshape(m, -1)
    dkv = dkv.reshape(b, nr, t, 2 * hd).transpose(1, 0, 2, 3).reshape(nr * m, 2 * hd)
    dkv_own = scatter(dkv, ("row", "col"))
    d_query = scatter(mm(dq, one, 0, 0).astype(BF), "row")
    e_one = scatter(mm(dq, wq, 1, 0).astype(BF), "col").astype(F32) + mm(dkv_own, wkv, 1, 1)
    normed1 = (x_own - mine(centre)) * mine(inverse)
    back_one, g_gain1, g_bias1 = norm_backward(e_one, normed1, mine(inverse), gain1, keep_own)
    grad_in = turn_back((grad_middle + back_one).astype(BF))
    d_kv = scatter(mm(one_own, dkv_own, 0, 0).astype(BF), "col")
    d_kv = lax.psum(d_kv, ("dp", "row")).astype(F32)
    small = lax.psum(jnp.stack([g_gain1, g_bias1, g_gain2, g_bias2]), ("dp", "row", "col"))
    small = lax.dynamic_slice_in_dim(small, col * f, f, 1)
    d_query = lax.psum(turn_back(d_query), "dp").astype(F32).T
    d_out = lax.psum(turn_back(d_out), "dp").astype(F32)
    d_up = gather(turn_back(d_up), "dp").astype(F32).T
    d_down = gather(turn_back(d_down), "dp").astype(F32)
    return (
        out.reshape(b, t, f),
        grad_in.reshape(b, t, f),
        small[0],
        small[1],
        d_query,
        d_kv,
        d_out,
        small[2],
        small[3],
        d_up,
        d_down,
    )


def solution(mesh):
    act, vec = (P("dp", "row", "col"), P("col"))
    wide, tall = (P("col", "row"), P("row", "col"))
    return jax.shard_map(
        local,
        mesh=mesh,
        in_specs=(act, P("dp"), act, vec, vec, wide, P("col", None), tall, vec, vec, wide, tall),
        out_specs=(act, act, vec, vec, wide, P("col", None), tall, vec, vec, wide, tall),
        check_vma=False,
    )
```

profile of v0, /device:TPU:0, one launch (start us, length us, event | category | flops | bytes accessed | tf_op | source)
XLA Modules:
  0.0 1477.3 jit_solution(9713727474657189356)
XLA Ops:
  10.0 13.0 all_to_all.200
  24.2 5.3 all_gather.40
  29.6 17.6 %all-gather.13.cloned.1.call-done = bf16[1024,2048]{1,0:T(8,128)(2,1)} async-done(((bf16[1024,512]{1,0:T(8,128)(2,1)}), bf16[1024,2048]{1,0:T(8,128)(2,1)}) %all-gather.13.cloned.1.call-update) | async-done | bytes 4194320 | tf_op jit(solution)/shard_map/all_gather | solution.py:43
  47.2 3.6 convert_reduce_fusion
  50.8 7.5 fusion.11
  58.3 7.5 all-gather.17.cloned.1.call-done
  68.4 3.5 all-to-all-start.1
  73.9 6.9 all-to-all-done.1
  82.3 31.9 %all-gather.15.cloned.1.call-done = bf16[512,2048]{0,1:T(8,128)(2,1)} async-done(((bf16[128,2048]{0,1:T(8,128)(2,1)}), bf16[512,2048]{0,1:T(8,128)(2,1)}) %all-gather.15.cloned.1.call-update) | async-done | bytes 2097168 | tf_op jit(solution)/shard_map/all_gather | solution.py:43
  114.2 5.2 convolution_convert_fusion.10
  119.4 37.1 %all-gather.19.cloned.1.call-done = bf16[4096,256]{1,0:T(8,128)(2,1)} async-done(((bf16[256,256]{1,0:T(8,128)(2,1)}), bf16[4096,256]{1,0:T(8,128)(2,1)}) %all-gather.19.cloned.1.call-update) | async-done | bytes 2097168 | tf_op jit(solution)/shard_map/all_gather | solution.py:43
  184.7 18.8 %all-gather.21.cloned.1.call-done = bf16[512,2048]{0,1:T(8,128)(2,1)} async-done(((bf16[128,2048]{0,1:T(8,128)(2,1)}), bf16[512,2048]{0,1:T(8,128)(2,1)}) %all-gather.21.cloned.1.call-update) | async-done | bytes 2097168 | tf_op jit(solution)/shard_map/all_gather | solution.py:43
  203.5 6.3 convolution_convert_fusion.5
  210.0 17.2 %all_to_all.201 = bf16[4,256,512]{2,1,0:T(8,128)(2,1)S(1)} all-to-all(bf16[4,256,512]{2,1,0:T(8,128)(2,1)S(1)} %bitcast.406), channel_id=1, replica_groups=mesh['dp'=2,'row'=4,'col'=4] {'col'}, dimensions={0} | all-to-all | bytes 2097152 | tf_op jit(solution)/shard_map/all_to_all | solution.py:35
  229.1 28.4 %all_to_all.202 = bf16[4,256,512]{2,1,0:T(8,128)(2,1)S(1)} all-to-all(bf16[4,256,512]{2,1,0:T(8,128)(2,1)S(1)} %fusion.58), channel_id=1, replica_groups=mesh['dp'=2,'row'=4,'col'=4] {'col'}, dimensions={0} | all-to-all | bytes 2097152 | tf_op jit(solution)/shard_map/all_to_all | solution.py:35
  260.6 16.9 %all_to_all.203 = bf16[4,256,512]{2,1,0:T(8,128)(2,1)S(1)} all-to-all(bf16[4,256,512]{2,1,0:T(8,128)(2,1)S(1)} %bitcast.413), channel_id=1, replica_groups=mesh['dp'=2,'row'=4,'col'=4] {'col'}, dimensions={0} | all-to-all | bytes 2097152 | tf_op jit(solution)/shard_map/all_to_all | solution.py:35
  281.1 3.7 multiply_convert_fusion.10
  284.8 62.0 %all-gather.27.cloned.1.call-done = bf16[1024,2048]{0,1:T(8,128)(2,1)} async-done(((bf16[256,2048]{0,1:T(8,128)(2,1)}), bf16[1024,2048]{0,1:T(8,128)(2,1)}) %all-gather.27.cloned.1.call-update) | async-done | bytes 4194320 | tf_op jit(solution)/shard_map/all_gather | solution.py:43
  346.8 55.2 %all-gather.29.cloned.1.call-done = bf16[2048,2048]{1,0:T(8,128)(2,1)} async-done(((bf16[256,2048]{1,0:T(8,128)(2,1)}), bf16[2048,2048]{1,0:T(8,128)(2,1)}) %all-gather.29.cloned.1.call-update) | async-done | bytes 8388624 | tf_op jit(solution)/shard_map/all_gather | solution.py:43
  402.0 14.5 fusion.125
  416.4 67.8 %all-gather.25.cloned.1.call-done = bf16[1024,2048]{0,1:T(8,128)(2,1)} async-done(((bf16[256,2048]{0,1:T(8,128)(2,1)}), bf16[1024,2048]{0,1:T(8,128)(2,1)}) %all-gather.25.cloned.1.call-update) | async-done | bytes 4194320 | tf_op jit(solution)/shard_map/all_gather | solution.py:43
  484.2 55.1 %all-gather.23.cloned.1.call-done = bf16[2048,2048]{1,0:T(8,128)(2,1)} async-done(((bf16[256,2048]{1,0:T(8,128)(2,1)}), bf16[2048,2048]{1,0:T(8,128)(2,1)}) %all-gather.23.cloned.1.call-update) | async-done | bytes 8388624 | tf_op jit(solution)/shard_map/all_gather | solution.py:43
  539.3 22.2 %fusion.6 = (bf16[2048,1024]{1,0:T(8,128)(2,1)S(1)}, f32[2048,1024]{1,0:T(8,128)}) fusion(f32[2048,1024]{1,0:T(8,128)} %fusion.125, bf16[2048,2048]{1,0:T(8,128)(2,1)} %all-gather.23.cloned.1.call-done, bf16[1024,2048]{0,1:T(8,128)(2,1)} %all-gather.25.cloned.1.call-done), kind=kOutput, calls=%fused_computation.11 | convolution fusion | flops 8631877632 | bytes 33554432 | tf_op jit(solution)/shard_map/dot_general | solution.py:12
  563.5 11.0 convolution_convert_fusion
  574.5 15.4 %convolution_convert_fusion.1 = bf16[2048,2048]{1,0:T(8,128)(2,1)} fusion(bf16[1024,2048]{0,1:T(8,128)(2,1)} %all-gather.27.cloned.1.call-done, f32[2048,1024]{1,0:T(8,128)} %get-tuple-element.69), kind=kOutput, calls=%fused_computation.20 | convolution fusion | flops 8613003264 | bytes 20971520 | tf_op jit(solution)/shard_map/dot_general | solution.py:12
  590.0 55.9 %reduce-scatter.15.cloned.1.call-done = bf16[256,2048]{1,0:T(8,128)(2,1)} async-done(((bf16[2048,2048]{1,0:T(8,128)(2,1)}), bf16[256,2048]{1,0:T(8,128)(2,1)}) %reduce-scatter.15.cloned.1.call-update) | async-done | bytes 1048592 | tf_op jit(solution)/shard_map/reduce_scatter | solution.py:47
  648.7 71.8 %reduce-scatter.13.cloned.1.call-done = bf16[256,2048]{1,0:T(8,128)(2,1)} async-done(((bf16[2048,2048]{1,0:T(8,128)(2,1)}), bf16[256,2048]{1,0:T(8,128)(2,1)}) %reduce-scatter.13.cloned.1.call-update) | async-done | bytes 1048592 | tf_op jit(solution)/shard_map/reduce_scatter | solution.py:47
  720.5 5.3 fusion.111
  725.9 34.5 %all-gather.31.cloned.1.call-done = bf16[1024,2048]{1,0:T(8,128)(2,1)} async-done(((bf16[256,2048]{1,0:T(8,128)(2,1)}), bf16[1024,2048]{1,0:T(8,128)(2,1)}) %all-gather.31.cloned.1.call-update) | async-done | bytes 4194320 | tf_op jit(solution)/shard_map/all_gather | solution.py:43
  760.4 5.3 convolution_convert_fusion.9
  767.4 2.9 multiply_reduce_fusion.3
  774.3 3.0 multiply_reduce_fusion.2
  799.9 2.9 multiply_reduce_fusion.4
  804.8 4.4 multiply_convert_fusion.4
  812.1 4.4 multiply_convert_fusion.8
  818.9 3.1 multiply_convert_fusion.1
  822.0 3.8 multiply_convert_fusion.2
  825.8 3.8 multiply_convert_fusion.3
  849.0 16.0 %convolution_convert_fusion.2 = bf16[1024,2048]{1,0:T(8,128)(2,1)} fusion(bf16[2048,2048]{1,0:T(8,128)(2,1)} %all-gather.29.cloned.1.call-done, f32[2048,1024]{1,0:T(8,128)} %get-tuple-element.69), kind=kOutput, calls=%fused_computation.73 | convolution fusion | flops 8610906112 | bytes 20971520 | tf_op jit(solution)/shard_map/dot_general | solution.py:12
  865.3 14.2 convolution_convert_fusion.3
  892.1 6.0 convolution_convert_fusion.7
  898.5 5.9 convolution_convert_fusion.6
  904.4 6.3 reduce-scatter.19.cloned.1.call-done
  913.4 75.8 %reduce-scatter.29.cloned.1.call-done = bf16[256,2048]{1,0:T(8,128)(2,1)} async-done(((bf16[1024,2048]{1,0:T(8,128)(2,1)}), bf16[256,2048]{1,0:T(8,128)(2,1)}) %reduce-scatter.29.cloned.1.call-update) | async-done | bytes 1048592 | tf_op jit(solution)/shard_map/reduce_scatter | solution.py:47
  990.5 17.6 %all_to_all.204 = bf16[256,4,512]{2,0,1:T(8,128)(2,1)} all-to-all(bf16[256,4,512]{2,0,1:T(8,128)(2,1)S(1)} %bitcast.415), channel_id=1, replica_groups=mesh['dp'=2,'row'=4,'col'=4] {'col'}, dimensions={1} | all-to-all | bytes 2097152 | tf_op jit(solution)/shard_map/all_to_all | solution.py:39
  1008.2 6.0 convolution_convert_fusion.4
  1014.3 54.5 %reduce-scatter.27.cloned.1.call-done = bf16[256,2048]{1,0:T(8,128)(2,1)} async-done(((bf16[1024,2048]{1,0:T(8,128)(2,1)}), bf16[256,2048]{1,0:T(8,128)(2,1)}) %reduce-scatter.27.cloned.1.call-update) | async-done | bytes 1048592 | tf_op jit(solution)/shard_map/reduce_scatter | solution.py:47
  1070.1 17.0 %all_to_all.205 = bf16[256,4,512]{2,0,1:T(8,128)(2,1)S(1)} all-to-all(bf16[256,4,512]{2,0,1:T(8,128)(2,1)S(1)} %bitcast.416), channel_id=1, replica_groups=mesh['dp'=2,'row'=4,'col'=4] {'col'}, dimensions={1} | all-to-all | bytes 2097152 | tf_op jit(solution)/shard_map/all_to_all | solution.py:39
  1088.5 26.9 %reduce-scatter.21.cloned.1.call-done = bf16[128,2048]{1,0:T(8,128)(2,1)} async-done(((bf16[512,2048]{1,0:T(8,128)(2,1)}), bf16[128,2048]{1,0:T(8,128)(2,1)}) %reduce-scatter.21.cloned.1.call-update) | async-done | bytes 524304 | tf_op jit(solution)/shard_map/reduce_scatter | solution.py:47
  1117.2 3.5 all-to-all-start.7
  1120.7 40.1 %reduce-scatter.25.cloned.1.call-done = bf16[128,2048]{1,0:T(8,128)(2,1)} async-done(((bf16[512,2048]{1,0:T(8,128)(2,1)}), bf16[128,2048]{1,0:T(8,128)(2,1)}) %reduce-scatter.25.cloned.1.call-update) | async-done | bytes 524304 | tf_op jit(solution)/shard_map/reduce_scatter | solution.py:47
  1162.8 3.5 all-to-all-start.8
  1166.3 21.8 %reduce-scatter.23.cloned.1.call-done = bf16[512,256]{1,0:T(8,128)(2,1)} async-done(((bf16[2048,256]{1,0:T(8,128)(2,1)}), bf16[512,256]{1,0:T(8,128)(2,1)}) %reduce-scatter.23.cloned.1.call-update) | async-done | bytes 262160 | tf_op jit(solution)/shard_map/reduce_scatter | solution.py:47
  1189.6 33.1 %all-gather.35.cloned.1.call-done = bf16[2048,512]{1,0:T(8,128)(2,1)} async-done(((bf16[1024,512]{1,0:T(8,128)(2,1)}), bf16[2048,512]{1,0:T(8,128)(2,1)}) %all-gather.35.cloned.1.call-update) | async-done | bytes 2097168 | tf_op jit(solution)/shard_map/all_gather | solution.py:43
  1222.7 4.2 convert_element_type.337
  1229.0 3.6 all-to-all-start.4
  1233.2 37.7 %reduce-scatter.17.cloned.1.call-done = bf16[256,2048]{1,0:T(8,128)(2,1)} async-done(((bf16[1024,2048]{1,0:T(8,128)(2,1)}), bf16[256,2048]{1,0:T(8,128)(2,1)}) %reduce-scatter.17.cloned.1.call-update) | async-done | bytes 1048592 | tf_op jit(solution)/shard_map/reduce_scatter | solution.py:47
  1270.9 3.1 fusion.39
  1277.1 4.3 all-to-all-start.6
  1281.4 24.4 %all-gather.33.cloned.1.call-done = bf16[2048,512]{0,1:T(8,128)(2,1)} async-done(((bf16[1024,512]{0,1:T(8,128)(2,1)}), bf16[2048,512]{0,1:T(8,128)(2,1)}) %all-gather.33.cloned.1.call-update) | async-done | bytes 2097168 | tf_op jit(solution)/shard_map/all_gather | solution.py:43
  1305.8 4.3 convert_bitcast_fusion
  1310.1 69.8 %all-reduce.4.cloned.1.call-done = bf16[512,256]{1,0:T(8,128)(2,1)} async-done(((bf16[512,256]{1,0:T(8,128)(2,1)}), bf16[512,256]{1,0:T(8,128)(2,1)}) %all-reduce.4.cloned.1.call-update) | async-done | bytes 262160 | tf_op jit(solution)/shard_map/psum | solution.py:185
  1381.6 40.7 %all-reduce.6.cloned.1.call-done = (bf16[512,512]{1,0:T(8,128)(2,1)}, bf16[512,512]{1,0:T(8,128)(2,1)}) async-done(((bf16[512,512]{1,0:T(8,128)(2,1)}, bf16[512,512]{1,0:T(8,128)(2,1)}), (bf16[512,512]{1,0:T(8,128)(2,1)}, bf16[512,512]{1,0:T(8,128)(2,1)})) %all-reduce.6.cloned.1.call-update) | async-done | bytes 1048592 | tf_op jit(solution)/shard_map/psum | solution.py:188
  1426.6 39.5 %psum.28 = f32[4,2048]{1,0:T(4,128)S(1)} all-reduce(f32[4,2048]{1,0:T(4,128)S(1)} %pad_maximum_fusion.2), channel_id=1, replica_groups=mesh['dp'=2,'row'=4,'col'=4] {'dp','row','col'}, use_global_device_ids=true, to_apply=%region_41.42 | all-reduce | flops 8192 | bytes 65536 | tf_op jit(solution)/shard_map/psum | solution.py:186
  (304 shorter events, 147.1 us)
Async XLA Ops:
  7.2 202.7 %copy-start = (bf16[2048,512]{1,0:T(8,128)(2,1)S(1)}, bf16[2048,512]{1,0:T(8,128)(2,1)}, u32[]{:S(2)}) copy-start(bf16[2048,512]{1,0:T(8,128)(2,1)} %param.23) | copy-start | bytes 6291460
  7.2 16.9 %copy-start.53 = (s32[2]{0:T(128)S(1)}, s32[2]{0:T(128)}, u32[]{:S(2)}) copy-start(s32[2]{0:T(128)} %param.13) | copy-start | bytes 28
  7.2 17.0 %copy-start.54 = (f32[512]{0:T(512)S(1)}, f32[512]{0:T(512)}, u32[]{:S(2)}) copy-start(f32[512]{0:T(512)} %param.21) | copy-start | bytes 6148
  7.2 17.0 %copy-start.55 = (f32[512]{0:T(512)S(1)}, f32[512]{0:T(512)}, u32[]{:S(2)}) copy-start(f32[512]{0:T(512)} %param.20) | copy-start | bytes 6148
  7.2 17.0 %copy-start.56 = (f32[512]{0:T(512)S(1)}, f32[512]{0:T(512)}, u32[]{:S(2)}) copy-start(f32[512]{0:T(512)} %param.16) | copy-start | bytes 6148
  7.2 17.0 %copy-start.57 = (f32[512]{0:T(512)S(1)}, f32[512]{0:T(512)}, u32[]{:S(2)}) copy-start(f32[512]{0:T(512)} %param.15) | copy-start | bytes 6148
  7.2 39.9 %all-gather.13.cloned.1.call-start = ((), (), s32[]{:S(2)}) async-start(), calls=%async_computation.21 | async-start | bytes 5242880 | tf_op jit(solution)/shard_map/all_gather | solution.py:43
  8.0 57.8 %all-gather.17.cloned.1.call-start = ((), (), s32[]{:S(2)}) async-start(), calls=%async_computation.23 | async-start | bytes 1310720 | tf_op jit(solution)/shard_map/all_gather | solution.py:43
  8.7 105.5 %all-gather.15.cloned.1.call-start = ((), (), s32[]{:S(2)}) async-start(), calls=%async_computation.22 | async-start | bytes 2621440 | tf_op jit(solution)/shard_map/all_gather | solution.py:43
  24.0 132.5 %all-gather.19.cloned.1.call-start = ((), (), s32[]{:S(2)}) async-start(), calls=%async_computation.24 | async-start | bytes 2228224 | tf_op jit(solution)/shard_map/all_gather | solution.py:43
  29.6 28.7 %copy-start.49 = (f32[1,2048]{1,0:T(1,128)}, f32[1,2048]{1,0:T(1,128)S(1)}, u32[]{:S(2)}) copy-start(f32[1,2048]{1,0:T(1,128)S(1)} %get-tuple-element.32) | copy-start | bytes 24580
  50.8 7.5 copy-start.51
  50.8 7.5 copy-start.52
  68.4 12.3 all-to-all-start.1
  71.9 131.5 %all-gather.21.cloned.1.call-start = ((), (), s32[]{:S(2)}) async-start(), calls=%async_computation.25 | async-start | bytes 2621440 | tf_op jit(solution)/shard_map/all_gather | solution.py:43
  81.8 197.1 %reduce-scatter.11.cloned.1.call-start = ((), (), s32[]{:S(2)}) async-start(), calls=%async_computation.26 | async-start | bytes 5242880 | tf_op jit(solution)/shard_map/reduce_scatter | solution.py:47
  119.4 48.5 %copy-start.47 = (bf16[1024,512]{1,0:T(8,128)(2,1)}, bf16[1024,512]{1,0:T(8,128)(2,1)S(1)}, u32[]{:S(2)}) copy-start(bf16[1024,512]{1,0:T(8,128)(2,1)S(1)} %convolution_convert_fusion.10) | copy-start | bytes 3145732
  158.2 23.6 %copy-start.19 = (bf16[4,2,512,256]{3,2,0,1:T(8,128)(2,1)}, bf16[4,2,512,256]{3,2,0,1:T(8,128)(2,1)S(1)}, u32[]{:S(2)}) copy-start(bf16[4,2,512,256]{3,2,0,1:T(8,128)(2,1)S(1)} %copy.68) | copy-start | bytes 6291460
  159.6 15.7 %copy-start.12 = (f32[512,2048]{1,0:T(8,128)}, f32[512,2048]{1,0:T(8,128)S(1)}, u32[]{:S(2)}) copy-start(f32[512,2048]{1,0:T(8,128)S(1)} %get-tuple-element.53) | copy-start | bytes 12582916
  161.0 15.2 %copy-start.10 = (f32[512,2048]{1,0:T(8,128)}, f32[512,2048]{1,0:T(8,128)S(1)}, u32[]{:S(2)}) copy-start(f32[512,2048]{1,0:T(8,128)S(1)} %get-tuple-element.55) | copy-start | bytes 12582916
  162.4 14.8 copy-start.8
  163.8 14.3 copy-start.14
  165.2 13.8 copy-start.6
  166.5 13.4 copy-start.4
  167.9 12.9 copy-start.2
  169.5 12.3 copy-start.16
  209.8 19.0 %copy-start.45 = (bf16[2,512,512]{2,1,0:T(8,128)(2,1)S(1)}, bf16[2,512,512]{2,1,0:T(8,128)(2,1)}, u32[]{:S(2)}) copy-start(bf16[2,512,512]{2,1,0:T(8,128)(2,1)} %param.14) | copy-start | bytes 3145732
  209.8 136.9 %all-gather.27.cloned.1.call-start = ((), (), s32[]{:S(2)}) async-start(), calls=%async_computation.29 | async-start | bytes 5242880 | tf_op jit(solution)/shard_map/all_gather | solution.py:43
  228.5 173.5 %all-gather.29.cloned.1.call-start = ((), (), s32[]{:S(2)}) async-start(), calls=%async_computation.31 | async-start | bytes 9437184 | tf_op jit(solution)/shard_map/all_gather | solution.py:43
  258.7 225.6 %all-gather.25.cloned.1.call-start = ((), (), s32[]{:S(2)}) async-start(), calls=%async_computation.28 | async-start | bytes 5242880 | tf_op jit(solution)/shard_map/all_gather | solution.py:43
  278.8 260.5 %all-gather.23.cloned.1.call-start = ((), (), s32[]{:S(2)}) async-start(), calls=%async_computation.27 | async-start | bytes 9437184 | tf_op jit(solution)/shard_map/all_gather | solution.py:43
  284.7 361.2 %reduce-scatter.15.cloned.1.call-start = ((), (), s32[]{:S(2)}) async-start(), calls=%async_computation.32 | async-start | bytes 9437184 | tf_op jit(solution)/shard_map/reduce_scatter | solution.py:47
  539.3 24.1 %copy-start.58 = (bf16[1024,2048]{0,1:T(8,128)(2,1)S(1)}, bf16[1024,2048]{0,1:T(8,128)(2,1)}, u32[]{:S(2)}) copy-start(bf16[1024,2048]{0,1:T(8,128)(2,1)} %all-gather.25.cloned.1.call-done) | copy-start | bytes 12582916
  574.5 146.1 %reduce-scatter.13.cloned.1.call-start = ((), (), s32[]{:S(2)}) async-start(), calls=%async_computation.30 | async-start | bytes 9437184 | tf_op jit(solution)/shard_map/reduce_scatter | solution.py:47
  589.9 56.0 %copy-start.38 = (bf16[256,2048]{1,0:T(8,128)(2,1)S(1)}, bf16[256,2048]{1,0:T(8,128)(2,1)}, u32[]{:S(2)}) copy-start(bf16[256,2048]{1,0:T(8,128)(2,1)} %reduce-scatter.11.cloned.1.call-done) | copy-start | bytes 3145732
  589.9 130.6 %copy-start.39 = (bf16[4,32,8,512]{3,2,0,1:T(8,128)(2,1)S(1)}, bf16[4,32,8,512]{3,2,0,1:T(8,128)(2,1)}, u32[]{:S(2)}) copy-start(bf16[4,32,8,512]{3,2,0,1:T(8,128)(2,1)} %copy.95) | copy-start | bytes 3145732
  589.9 170.5 %all-gather.31.cloned.1.call-start = ((), (), s32[]{:S(2)}) async-start(), calls=%async_computation.33 | async-start | bytes 5242880 | tf_op jit(solution)/shard_map/all_gather | solution.py:43
  725.8 184.9 %reduce-scatter.19.cloned.1.call-start = ((), (), s32[]{:S(2)}) async-start(), calls=%async_computation.35 | async-start | bytes 2228224 | tf_op jit(solution)/shard_map/reduce_scatter | solution.py:47
  760.4 5.3 copy-start.15
  822.0 11.4 copy-start.25
  825.8 5.7 copy-start.26
  836.2 9.4 copy-start.29
  849.0 140.3 %reduce-scatter.29.cloned.1.call-start = ((), (), s32[]{:S(2)}) async-start(), calls=%async_computation.42 | async-start | bytes 5242880 | tf_op jit(solution)/shard_map/reduce_scatter | solution.py:47
  865.0 203.8 %reduce-scatter.27.cloned.1.call-start = ((), (), s32[]{:S(2)}) async-start(), calls=%async_computation.40 | async-start | bytes 5242880 | tf_op jit(solution)/shard_map/reduce_scatter | solution.py:47
  879.6 235.8 %reduce-scatter.21.cloned.1.call-start = ((), (), s32[]{:S(2)}) async-start(), calls=%async_computation.36 | async-start | bytes 2621440 | tf_op jit(solution)/shard_map/reduce_scatter | solution.py:47
  881.1 5.2 copy-start.28
  881.1 6.0 copy-start.24
  892.1 6.3 copy-start.46
  898.1 262.6 %reduce-scatter.25.cloned.1.call-start = ((), (), s32[]{:S(2)}) async-start(), calls=%async_computation.39 | async-start | bytes 2621440 | tf_op jit(solution)/shard_map/reduce_scatter | solution.py:47
  904.3 283.8 %reduce-scatter.23.cloned.1.call-start = ((), (), s32[]{:S(2)}) async-start(), calls=%async_computation.37 | async-start | bytes 1310720 | tf_op jit(solution)/shard_map/reduce_scatter | solution.py:47
  913.4 309.3 %all-gather.35.cloned.1.call-start = ((), (), s32[]{:S(2)}) async-start(), calls=%async_computation.43 | async-start | bytes 3145728 | tf_op jit(solution)/shard_map/all_gather | solution.py:43
  1008.2 262.7 %reduce-scatter.17.cloned.1.call-start = ((), (), s32[]{:S(2)}) async-start(), calls=%async_computation.34 | async-start | bytes 5242880 | tf_op jit(solution)/shard_map/reduce_scatter | solution.py:47
  1014.2 291.6 %all-gather.33.cloned.1.call-start = ((), (), s32[]{:S(2)}) async-start(), calls=%async_computation.41 | async-start | bytes 3145728 | tf_op jit(solution)/shard_map/all_gather | solution.py:43
  1117.2 45.6 %all-to-all-start.7 = ((bf16[128,4,512]{2,0,1:T(8,128)(2,1)}), bf16[128,4,512]{2,0,1:T(8,128)(2,1)S(1)}, u32[]{:S(2)}, u32[]{:S(2)}) async-start(bf16[128,4,512]{2,0,1:T(8,128)(2,1)} %bitcast.354), calls=%async_computation.13 | async-start | bytes 1048576 | tf_op jit(solution)/shard_map/all_to_all | solution.py:39
  1160.8 66.1 %copy-start.41 = (bf16[256,2048]{1,0:T(8,128)(2,1)S(1)}, bf16[256,2048]{1,0:T(8,128)(2,1)}, u32[]{:S(2)}) copy-start(bf16[256,2048]{1,0:T(8,128)(2,1)} %get-tuple-element.27) | copy-start | bytes 3145732
  1162.8 66.2 %all-to-all-start.8 = ((bf16[128,4,512]{2,0,1:T(8,128)(2,1)}), bf16[128,4,512]{2,0,1:T(8,128)(2,1)S(1)}, u32[]{:S(2)}, u32[]{:S(2)}) async-start(bf16[128,4,512]{2,0,1:T(8,128)(2,1)} %bitcast.353), calls=%async_computation.16 | async-start | bytes 1048576 | tf_op jit(solution)/shard_map/all_to_all | solution.py:39
  1166.2 213.6 %all-reduce.4.cloned.1.call-start = ((), (), s32[]{:S(2)}) async-start(), calls=%async_computation.38 | async-start | bytes 524288 | tf_op jit(solution)/shard_map/psum | solution.py:185
  1226.9 44.0 %copy-start.48 = (bf16[256,256]{1,0:T(8,128)(2,1)S(1)}, bf16[256,256]{1,0:T(8,128)(2,1)}, u32[]{:S(2)}) copy-start(bf16[256,256]{1,0:T(8,128)(2,1)} %reduce-scatter.19.cloned.1.call-done) | copy-start | bytes 393220
  1226.9 44.0 %copy-start.50 = (f32[1,2048]{1,0:T(1,128)S(1)}, f32[1,2048]{1,0:T(1,128)}, u32[]{:S(2)}) copy-start(f32[1,2048]{1,0:T(1,128)} %copy-done.49) | copy-start | bytes 24580
  1229.0 48.1 %all-to-all-start.4 = ((bf16[256,4,512]{2,0,1:T(8,128)(2,1)}), bf16[256,4,512]{2,0,1:T(8,128)(2,1)S(1)}, u32[]{:S(2)}, u32[]{:S(2)}) async-start(bf16[256,4,512]{2,0,1:T(8,128)(2,1)} %bitcast.352), calls=%async_computation.6 | async-start | bytes 2097152 | tf_op jit(solution)/shard_map/all_to_all | solution.py:39
  1232.6 189.7 %all-reduce.6.cloned.1.call-start = ((), (), s32[]{:S(2)}) async-start(), calls=%async_computation.44 | async-start | bytes 2097152 | tf_op jit(solution)/shard_map/psum | solution.py:188
  1232.7 41.3 %copy-start.40 = (f32[256,2048]{1,0:T(8,128)S(1)}, f32[256,2048]{1,0:T(8,128)}, u32[]{:S(2)}) copy-start(f32[256,2048]{1,0:T(8,128)} %get-tuple-element.26) | copy-start | bytes 6291460
  1277.1 189.7 %all-to-all-start.6 = ((bf16[256,4,512]{2,0,1:T(8,128)(2,1)}), bf16[256,4,512]{2,0,1:T(8,128)(2,1)}, u32[]{:S(2)}, u32[]{:S(2)}) async-start(bf16[256,4,512]{2,0,1:T(8,128)(2,1)} %bitcast.351), calls=%async_computation.11 | async-start | bytes 2097152 | tf_op jit(solution)/shard_map/all_to_all | solution.py:39
  1305.8 164.3 %copy-start.1 = (bf16[2048,512]{1,0:T(8,128)(2,1)S(1)}, bf16[2048,512]{1,0:T(8,128)(2,1)}, u32[]{:S(2)}) copy-start(bf16[2048,512]{1,0:T(8,128)(2,1)} %param.23) | copy-start | bytes 6291460
  (25 other events, 72.8 us)
Sparse Core Ops, SparseCore 0:
  9.6 37.4 all-gather.12
  48.7 17.0 all-gather.16
  67.9 46.2 all-gather.14
  116.8 39.6 all-gather.18
  158.4 44.9 all-gather.20
  209.9 53.9 reduce-scatter.10
  266.2 80.5 all-gather.26
  349.4 52.5 all-gather.28
  403.6 80.5 all-gather.24
  486.7 52.5 all-gather.22
  574.6 71.3 reduce-scatter.14
  649.2 71.2 reduce-scatter.12
  725.9 34.4 all-gather.30
  849.1 61.5 reduce-scatter.18
  913.4 75.7 reduce-scatter.28
  991.5 77.2 reduce-scatter.26
  1070.9 44.3 reduce-scatter.20
  1117.6 43.1 reduce-scatter.24
  1163.9 24.1 reduce-scatter.22
  1189.6 33.1 all-gather.34
  1226.0 44.8 reduce-scatter.16
  1273.0 32.7 all-gather.32
  1309.2 70.6 all-reduce.3
  1382.7 39.5 all-reduce.5
where the time goes:
time: 1480 us
  waiting for transfers between devices  955 us (65%)
  matrix products  214 us (14%)
  blocking collectives  155 us (10%)
  other arithmetic  73.4 us (5%)
  local copies, waits for them, and re-layouts  43.2 us (3%)
  starting transfers between devices  20.2 us (1%)
  between operations  16 us (1%)
    all_gather x12, waiting for transfers between devices, gather(): return lax.all_gather(x, axes, axis=dim, tiled=True)  445 us
    reduce_scatter x10, waiting for transfers between devices, scatter(): return lax.psum_scatter(x, axes, scatter_dimension=0, tiled=True)  391 us
    dot_general x63, matrix products, mm(): lax.dot_general(a, b, (((ca,), (cb,)), ((), ())), preferred_element_type=...  214 us
    all_to_all x4, blocking collectives, turn(): return lax.all_to_all(weight, 'col', 0, 1, tiled=True)  75.5 us
    psum x1, waiting for transfers between devices, local(): d_kv = lax.psum(d_kv, ('dp', 'row')).astype(F32)  69.8 us
    psum x1, waiting for transfers between devices, local(): d_query = lax.psum(turn_back(d_query), 'dp').astype(F32).T  40.7 us
    psum x1, blocking collectives, local(): lax.psum(jnp.stack([g_gain1, g_bias1, g_gain2, g_bias2]), ('dp', 'row', '...  39.5 us
    all_to_all x2, blocking collectives, turn_back(): return lax.all_to_all(rows, 'col', 1, 0, tiled=True)  34.6 us
  transfers between devices with their start and end apart: 29, of which 24 were waited for; matrix products, arithmetic and copies ran while one was open for 13% of the time, Pallas kernels for 0%

commit v1 on v0

--- a/solution.py
+++ b/solution.py
@@ -36,7 +36,10 @@
 
 
 def turn_back(rows):
-    return lax.all_to_all(rows, "col", 1, 0, tiled=True)
+    return jnp.concatenate(
+        lax.all_to_all(jnp.stack(jnp.split(rows, lax.axis_size("col"), axis=1)), "col", 0, 0),
+        axis=0,
+    )
 
 
 def gather(x, axes, dim=0):

time: 1480 us -> 1410 us (0.953)
  waiting for transfers between devices: 955 us -> 880 us
    reduce_scatter x10, waiting for transfers between devices: 391 us -> 331 us  [scatter(): return lax.psum_scatter(x, axes, scatter_dimension=0, tiled=True)]
    all_gather x12, waiting for transfers between devices: 445 us -> 423 us  [gather(): return lax.all_gather(x, axes, axis=dim, tiled=True)]
  transfers between devices with their start and end apart: 29 -> 29, of which waited for: 24 -> 24; matrix products, arithmetic and copies ran while one was open for 13% -> 20% of each run, Pallas kernels for 0% -> 0%
where the time goes in v1:
time: 1410 us
  waiting for transfers between devices  880 us (62%)
  matrix products  219 us (16%)
  blocking collectives  156 us (11%)
  other arithmetic  78.9 us (6%)
  local copies, waits for them, and re-layouts  35.6 us (3%)
  starting transfers between devices  20.2 us (1%)
  between operations  15.9 us (1%)
    all_gather x12, waiting for transfers between devices, gather(): return lax.all_gather(x, axes, axis=dim, tiled=True)  423 us
    reduce_scatter x10, waiting for transfers between devices, scatter(): return lax.psum_scatter(x, axes, scatter_dimension=0, tiled=True)  331 us
    dot_general x63, matrix products, mm(): lax.dot_general(a, b, (((ca,), (cb,)), ((), ())), preferred_element_type=...  219 us
    all_to_all x4, blocking collectives, turn(): return lax.all_to_all(weight, 'col', 0, 1, tiled=True)  75.5 us
    psum x1, waiting for transfers between devices, local(): d_kv = lax.psum(d_kv, ('dp', 'row')).astype(F32)  69.7 us
    psum x1, waiting for transfers between devices, local(): d_query = lax.psum(turn_back(d_query), 'dp').astype(F32).T  40.7 us
    psum x1, blocking collectives, local(): lax.psum(jnp.stack([g_gain1, g_bias1, g_gain2, g_bias2]), ('dp', 'row', '...  39.5 us
    all_to_all x2, blocking collectives, turn_back(): lax.all_to_all(jnp.stack(jnp.split(rows, lax.axis_size('col'), axis=1)),...  36.1 us
  transfers between devices with their start and end apart: 29, of which 24 were waited for; matrix products, arithmetic and copies ran while one was open for 20% of the time, Pallas kernels for 0%

profile of v1, /device:TPU:0, one launch (start us, length us, event | category | flops | bytes accessed | tf_op | source)
XLA Modules:
  0.0 1405.7 jit_solution(7785542995526260991)
XLA Ops:
  10.0 13.0 all_to_all.122
  24.2 5.3 all_gather.40
  29.6 17.6 %all-gather.13.cloned.1.call-done = bf16[1024,2048]{1,0:T(8,128)(2,1)} async-done(((bf16[1024,512]{1,0:T(8,128)(2,1)}), bf16[1024,2048]{1,0:T(8,128)(2,1)}) %all-gather.13.cloned.1.call-update) | async-done | bytes 4194320 | tf_op jit(solution)/shard_map/all_gather | solution.py:46
  47.2 3.6 convert_reduce_fusion
  50.8 7.5 fusion.11
  58.3 7.5 all-gather.17.cloned.1.call-done
  68.4 3.5 all-to-all-start.1
  73.9 6.9 all-to-all-done.1
  82.4 31.9 %all-gather.15.cloned.1.call-done = bf16[512,2048]{0,1:T(8,128)(2,1)} async-done(((bf16[128,2048]{0,1:T(8,128)(2,1)}), bf16[512,2048]{0,1:T(8,128)(2,1)}) %all-gather.15.cloned.1.call-update) | async-done | bytes 2097168 | tf_op jit(solution)/shard_map/all_gather | solution.py:46
  114.2 5.2 convolution_convert_fusion.10
  119.4 37.0 %all-gather.19.cloned.1.call-done = bf16[4096,256]{1,0:T(8,128)(2,1)} async-done(((bf16[256,256]{1,0:T(8,128)(2,1)}), bf16[4096,256]{1,0:T(8,128)(2,1)}) %all-gather.19.cloned.1.call-update) | async-done | bytes 2097168 | tf_op jit(solution)/shard_map/all_gather | solution.py:46
  184.7 18.8 %all-gather.21.cloned.1.call-done = bf16[512,2048]{0,1:T(8,128)(2,1)} async-done(((bf16[128,2048]{0,1:T(8,128)(2,1)}), bf16[512,2048]{0,1:T(8,128)(2,1)}) %all-gather.21.cloned.1.call-update) | async-done | bytes 2097168 | tf_op jit(solution)/shard_map/all_gather | solution.py:46
  203.5 6.3 convolution_convert_fusion.5
  210.0 17.2 %all_to_all.123 = bf16[4,256,512]{2,1,0:T(8,128)(2,1)S(1)} all-to-all(bf16[4,256,512]{2,1,0:T(8,128)(2,1)S(1)} %bitcast.418), channel_id=1, replica_groups=mesh['dp'=2,'row'=4,'col'=4] {'col'}, dimensions={0} | all-to-all | bytes 2097152 | tf_op jit(solution)/shard_map/all_to_all | solution.py:35
  229.1 28.4 %all_to_all.124 = bf16[4,256,512]{2,1,0:T(8,128)(2,1)S(1)} all-to-all(bf16[4,256,512]{2,1,0:T(8,128)(2,1)S(1)} %fusion.58), channel_id=1, replica_groups=mesh['dp'=2,'row'=4,'col'=4] {'col'}, dimensions={0} | all-to-all | bytes 2097152 | tf_op jit(solution)/shard_map/all_to_all | solution.py:35
  260.6 16.9 %all_to_all.125 = bf16[4,256,512]{2,1,0:T(8,128)(2,1)S(1)} all-to-all(bf16[4,256,512]{2,1,0:T(8,128)(2,1)S(1)} %bitcast.425), channel_id=1, replica_groups=mesh['dp'=2,'row'=4,'col'=4] {'col'}, dimensions={0} | all-to-all | bytes 2097152 | tf_op jit(solution)/shard_map/all_to_all | solution.py:35
  281.1 3.7 multiply_convert_fusion.10
  284.8 62.0 %all-gather.27.cloned.1.call-done = bf16[1024,2048]{0,1:T(8,128)(2,1)} async-done(((bf16[256,2048]{0,1:T(8,128)(2,1)}), bf16[1024,2048]{0,1:T(8,128)(2,1)}) %all-gather.27.cloned.1.call-update) | async-done | bytes 4194320 | tf_op jit(solution)/shard_map/all_gather | solution.py:46
  346.8 55.2 %all-gather.29.cloned.1.call-done = bf16[2048,2048]{1,0:T(8,128)(2,1)} async-done(((bf16[256,2048]{1,0:T(8,128)(2,1)}), bf16[2048,2048]{1,0:T(8,128)(2,1)}) %all-gather.29.cloned.1.call-update) | async-done | bytes 8388624 | tf_op jit(solution)/shard_map/all_gather | solution.py:46
  402.0 14.4 %fusion.125 = f32[2048,1024]{1,0:T(8,128)} fusion(bf16[2048,2048]{1,0:T(8,128)(2,1)} %all-gather.29.cloned.1.call-done, bf16[1024,2048]{0,1:T(8,128)(2,1)} %all-gather.27.cloned.1.call-done), kind=kOutput, calls=%fused_computation.305 | convolution fusion | flops 8589934592 | bytes 20971520 | tf_op jit(solution)/shard_map/dot_general | solution.py:12
  416.4 67.8 %all-gather.25.cloned.1.call-done = bf16[1024,2048]{0,1:T(8,128)(2,1)} async-done(((bf16[256,2048]{0,1:T(8,128)(2,1)}), bf16[1024,2048]{0,1:T(8,128)(2,1)}) %all-gather.25.cloned.1.call-update) | async-done | bytes 4194320 | tf_op jit(solution)/shard_map/all_gather | solution.py:46
  484.2 55.1 %all-gather.23.cloned.1.call-done = bf16[2048,2048]{1,0:T(8,128)(2,1)} async-done(((bf16[256,2048]{1,0:T(8,128)(2,1)}), bf16[2048,2048]{1,0:T(8,128)(2,1)}) %all-gather.23.cloned.1.call-update) | async-done | bytes 8388624 | tf_op jit(solution)/shard_map/all_gather | solution.py:46
  539.3 22.2 %fusion.6 = (bf16[2048,1024]{1,0:T(8,128)(2,1)S(1)}, f32[2048,1024]{1,0:T(8,128)}) fusion(f32[2048,1024]{1,0:T(8,128)} %fusion.125, bf16[2048,2048]{1,0:T(8,128)(2,1)} %all-gather.23.cloned.1.call-done, bf16[1024,2048]{0,1:T(8,128)(2,1)} %all-gather.25.cloned.1.call-done), kind=kOutput, calls=%fused_computation.11 | convolution fusion | flops 8631877632 | bytes 33554432 | tf_op jit(solution)/shard_map/dot_general | solution.py:12
  563.4 11.0 convolution_convert_fusion
  574.5 15.4 %convolution_convert_fusion.1 = bf16[2048,2048]{1,0:T(8,128)(2,1)} fusion(bf16[1024,2048]{0,1:T(8,128)(2,1)} %all-gather.27.cloned.1.call-done, f32[2048,1024]{1,0:T(8,128)} %get-tuple-element.93), kind=kOutput, calls=%fused_computation.20 | convolution fusion | flops 8613003264 | bytes 20971520 | tf_op jit(solution)/shard_map/dot_general | solution.py:12
  589.9 56.0 %reduce-scatter.15.cloned.1.call-done = bf16[256,2048]{1,0:T(8,128)(2,1)} async-done(((bf16[2048,2048]{1,0:T(8,128)(2,1)}), bf16[256,2048]{1,0:T(8,128)(2,1)}) %reduce-scatter.15.cloned.1.call-update) | async-done | bytes 1048592 | tf_op jit(solution)/shard_map/reduce_scatter | solution.py:50
  648.7 71.8 %reduce-scatter.13.cloned.1.call-done = bf16[256,2048]{1,0:T(8,128)(2,1)} async-done(((bf16[2048,2048]{1,0:T(8,128)(2,1)}), bf16[256,2048]{1,0:T(8,128)(2,1)}) %reduce-scatter.13.cloned.1.call-update) | async-done | bytes 1048592 | tf_op jit(solution)/shard_map/reduce_scatter | solution.py:50
  720.5 5.3 fusion.111
  725.9 16.1 %convolution_convert_fusion.2 = bf16[1024,2048]{1,0:T(8,128)(2,1)} fusion(bf16[2048,2048]{1,0:T(8,128)(2,1)} %all-gather.29.cloned.1.call-done, f32[2048,1024]{1,0:T(8,128)} %get-tuple-element.93), kind=kOutput, calls=%fused_computation.73 | convolution fusion | flops 8610906112 | bytes 20971520 | tf_op jit(solution)/shard_map/dot_general | solution.py:12
  742.3 18.1 %all-gather.31.cloned.1.call-done = bf16[1024,2048]{1,0:T(8,128)(2,1)} async-done(((bf16[256,2048]{1,0:T(8,128)(2,1)}), bf16[1024,2048]{1,0:T(8,128)(2,1)}) %all-gather.31.cloned.1.call-update) | async-done | bytes 4194320 | tf_op jit(solution)/shard_map/all_gather | solution.py:46
  760.4 5.3 convolution_convert_fusion.9
  765.8 3.1 multiply_reduce_fusion
  781.5 3.7 multiply_reduce_fusion.7
  785.3 4.5 multiply_convert_fusion.1
  789.7 4.5 multiply_convert_fusion.2
  806.4 3.8 multiply_reduce_fusion.6
  816.7 4.0 multiply_reduce_fusion.5
  820.8 4.5 multiply_convert_fusion.6
  825.3 3.8 convolution_add_fusion.11
  829.1 4.0 multiply_reduce_fusion.4
  833.1 4.5 multiply_convert_fusion.5
  850.9 14.1 convolution_convert_fusion.3
  877.6 6.1 convolution_convert_fusion.7
  885.4 18.9 %all_to_all.126 = bf16[4,256,512]{2,1,0:T(8,128)(2,1)} all-to-all(bf16[4,256,512]{2,1,0:T(8,128)(2,1)S(1)} %pad_maximum_fusion.5), channel_id=1, replica_groups=mesh['dp'=2,'row'=4,'col'=4] {'col'}, dimensions={0} | all-to-all | bytes 2097152 | tf_op jit(solution)/shard_map/all_to_all | solution.py:40
  904.4 5.9 convolution_convert_fusion.6
  915.7 6.0 convolution_convert_fusion.4
  921.8 69.2 %reduce-scatter.27.cloned.1.call-done = bf16[256,2048]{1,0:T(8,128)(2,1)} async-done(((bf16[1024,2048]{1,0:T(8,128)(2,1)}), bf16[256,2048]{1,0:T(8,128)(2,1)}) %reduce-scatter.27.cloned.1.call-update) | async-done | bytes 1048592 | tf_op jit(solution)/shard_map/reduce_scatter | solution.py:50
  992.4 17.1 %all_to_all.127 = bf16[4,256,512]{2,1,0:T(8,128)(2,1)S(1)} all-to-all(bf16[4,256,512]{2,1,0:T(8,128)(2,1)S(1)} %pad_maximum_fusion.4), channel_id=1, replica_groups=mesh['dp'=2,'row'=4,'col'=4] {'col'}, dimensions={0} | all-to-all | bytes 2097152 | tf_op jit(solution)/shard_map/all_to_all | solution.py:40
  1010.9 26.7 %reduce-scatter.21.cloned.1.call-done = bf16[128,2048]{1,0:T(8,128)(2,1)} async-done(((bf16[512,2048]{1,0:T(8,128)(2,1)}), bf16[128,2048]{1,0:T(8,128)(2,1)}) %reduce-scatter.21.cloned.1.call-update) | async-done | bytes 524304 | tf_op jit(solution)/shard_map/reduce_scatter | solution.py:50
  1039.5 3.5 all-to-all-start.7
  1044.5 26.9 %all-gather.35.cloned.1.call-done = bf16[2048,512]{1,0:T(8,128)(2,1)} async-done(((bf16[1024,512]{1,0:T(8,128)(2,1)}), bf16[2048,512]{1,0:T(8,128)(2,1)}) %all-gather.35.cloned.1.call-update) | async-done | bytes 2097168 | tf_op jit(solution)/shard_map/all_gather | solution.py:46
  1071.5 4.2 convert_element_type.337
  1075.7 42.1 %reduce-scatter.25.cloned.1.call-done = bf16[128,2048]{1,0:T(8,128)(2,1)} async-done(((bf16[512,2048]{1,0:T(8,128)(2,1)}), bf16[128,2048]{1,0:T(8,128)(2,1)}) %reduce-scatter.25.cloned.1.call-update) | async-done | bytes 524304 | tf_op jit(solution)/shard_map/reduce_scatter | solution.py:50
  1119.8 25.2 %reduce-scatter.23.cloned.1.call-done = bf16[512,256]{1,0:T(8,128)(2,1)} async-done(((bf16[2048,256]{1,0:T(8,128)(2,1)}), bf16[512,256]{1,0:T(8,128)(2,1)}) %reduce-scatter.23.cloned.1.call-update) | async-done | bytes 262160 | tf_op jit(solution)/shard_map/reduce_scatter | solution.py:50
  1145.0 3.5 all-to-all-start.8
  1150.8 6.6 all-to-all-done.8
  1157.3 3.5 all-to-all-start.4
  1161.4 37.7 %reduce-scatter.17.cloned.1.call-done = bf16[256,2048]{1,0:T(8,128)(2,1)} async-done(((bf16[1024,2048]{1,0:T(8,128)(2,1)}), bf16[256,2048]{1,0:T(8,128)(2,1)}) %reduce-scatter.17.cloned.1.call-update) | async-done | bytes 1048592 | tf_op jit(solution)/shard_map/reduce_scatter | solution.py:50
  1205.5 4.3 all-to-all-start.6
  1209.8 24.6 %all-gather.33.cloned.1.call-done = bf16[2048,512]{0,1:T(8,128)(2,1)} async-done(((bf16[1024,512]{0,1:T(8,128)(2,1)}), bf16[2048,512]{0,1:T(8,128)(2,1)}) %all-gather.33.cloned.1.call-update) | async-done | bytes 2097168 | tf_op jit(solution)/shard_map/all_gather | solution.py:46
  1234.4 4.3 convert_bitcast_fusion
  1238.7 69.7 %all-reduce.4.cloned.1.call-done = bf16[512,256]{1,0:T(8,128)(2,1)} async-done(((bf16[512,256]{1,0:T(8,128)(2,1)}), bf16[512,256]{1,0:T(8,128)(2,1)}) %all-reduce.4.cloned.1.call-update) | async-done | bytes 262160 | tf_op jit(solution)/shard_map/psum | solution.py:188
  1310.2 40.7 %all-reduce.6.cloned.1.call-done = (bf16[512,512]{1,0:T(8,128)(2,1)}, bf16[512,512]{1,0:T(8,128)(2,1)}) async-done(((bf16[512,512]{1,0:T(8,128)(2,1)}, bf16[512,512]{1,0:T(8,128)(2,1)}), (bf16[512,512]{1,0:T(8,128)(2,1)}, bf16[512,512]{1,0:T(8,128)(2,1)})) %all-reduce.6.cloned.1.call-update) | async-done | bytes 1048592 | tf_op jit(solution)/shard_map/psum | solution.py:191
  1355.2 39.5 %psum.28 = f32[4,2048]{1,0:T(4,128)S(1)} all-reduce(f32[4,2048]{1,0:T(4,128)S(1)} %pad_maximum_fusion.8), channel_id=1, replica_groups=mesh['dp'=2,'row'=4,'col'=4] {'dp','row','col'}, use_global_device_ids=true, to_apply=%region_41.42 | all-reduce | flops 8192 | bytes 65536 | tf_op jit(solution)/shard_map/psum | solution.py:189
  (312 shorter events, 143.3 us)
Async XLA Ops:
  7.2 202.7 %copy-start = (bf16[2048,512]{1,0:T(8,128)(2,1)S(1)}, bf16[2048,512]{1,0:T(8,128)(2,1)}, u32[]{:S(2)}) copy-start(bf16[2048,512]{1,0:T(8,128)(2,1)} %param.23) | copy-start | bytes 6291460
  7.2 16.9 %copy-start.54 = (s32[2]{0:T(128)S(1)}, s32[2]{0:T(128)}, u32[]{:S(2)}) copy-start(s32[2]{0:T(128)} %param.13) | copy-start | bytes 28
  7.2 17.0 %copy-start.55 = (f32[512]{0:T(512)S(1)}, f32[512]{0:T(512)}, u32[]{:S(2)}) copy-start(f32[512]{0:T(512)} %param.21) | copy-start | bytes 6148
  7.2 17.0 %copy-start.56 = (f32[512]{0:T(512)S(1)}, f32[512]{0:T(512)}, u32[]{:S(2)}) copy-start(f32[512]{0:T(512)} %param.20) | copy-start | bytes 6148
  7.2 17.0 %copy-start.57 = (f32[512]{0:T(512)S(1)}, f32[512]{0:T(512)}, u32[]{:S(2)}) copy-start(f32[512]{0:T(512)} %param.16) | copy-start | bytes 6148
  7.2 17.0 %copy-start.58 = (f32[512]{0:T(512)S(1)}, f32[512]{0:T(512)}, u32[]{:S(2)}) copy-start(f32[512]{0:T(512)} %param.15) | copy-start | bytes 6148
  7.2 39.9 %all-gather.13.cloned.1.call-start = ((), (), s32[]{:S(2)}) async-start(), calls=%async_computation.21 | async-start | bytes 5242880 | tf_op jit(solution)/shard_map/all_gather | solution.py:46
  8.0 57.8 %all-gather.17.cloned.1.call-start = ((), (), s32[]{:S(2)}) async-start(), calls=%async_computation.23 | async-start | bytes 1310720 | tf_op jit(solution)/shard_map/all_gather | solution.py:46
  8.7 105.5 %all-gather.15.cloned.1.call-start = ((), (), s32[]{:S(2)}) async-start(), calls=%async_computation.22 | async-start | bytes 2621440 | tf_op jit(solution)/shard_map/all_gather | solution.py:46
  24.0 132.4 %all-gather.19.cloned.1.call-start = ((), (), s32[]{:S(2)}) async-start(), calls=%async_computation.24 | async-start | bytes 2228224 | tf_op jit(solution)/shard_map/all_gather | solution.py:46
  29.6 28.7 %copy-start.50 = (f32[1,2048]{1,0:T(1,128)}, f32[1,2048]{1,0:T(1,128)S(1)}, u32[]{:S(2)}) copy-start(f32[1,2048]{1,0:T(1,128)S(1)} %get-tuple-element.56) | copy-start | bytes 24580
  50.8 7.5 copy-start.52
  50.8 7.5 copy-start.53
  68.4 12.3 all-to-all-start.1
  71.9 131.5 %all-gather.21.cloned.1.call-start = ((), (), s32[]{:S(2)}) async-start(), calls=%async_computation.25 | async-start | bytes 2621440 | tf_op jit(solution)/shard_map/all_gather | solution.py:46
  81.8 197.1 %reduce-scatter.11.cloned.1.call-start = ((), (), s32[]{:S(2)}) async-start(), calls=%async_computation.26 | async-start | bytes 5242880 | tf_op jit(solution)/shard_map/reduce_scatter | solution.py:50
  119.4 48.5 %copy-start.48 = (bf16[1024,512]{1,0:T(8,128)(2,1)}, bf16[1024,512]{1,0:T(8,128)(2,1)S(1)}, u32[]{:S(2)}) copy-start(bf16[1024,512]{1,0:T(8,128)(2,1)S(1)} %convolution_convert_fusion.10) | copy-start | bytes 3145732
  158.2 23.6 %copy-start.19 = (bf16[4,2,512,256]{3,2,0,1:T(8,128)(2,1)}, bf16[4,2,512,256]{3,2,0,1:T(8,128)(2,1)S(1)}, u32[]{:S(2)}) copy-start(bf16[4,2,512,256]{3,2,0,1:T(8,128)(2,1)S(1)} %copy.56) | copy-start | bytes 6291460
  159.6 15.7 %copy-start.2 = (f32[512,2048]{1,0:T(8,128)}, f32[512,2048]{1,0:T(8,128)S(1)}, u32[]{:S(2)}) copy-start(f32[512,2048]{1,0:T(8,128)S(1)} %get-tuple-element.77) | copy-start | bytes 12582916
  161.0 15.2 %copy-start.6 = (f32[512,2048]{1,0:T(8,128)}, f32[512,2048]{1,0:T(8,128)S(1)}, u32[]{:S(2)}) copy-start(f32[512,2048]{1,0:T(8,128)S(1)} %get-tuple-element.79) | copy-start | bytes 12582916
  162.4 14.8 %copy-start.10 = (f32[512,2048]{1,0:T(8,128)}, f32[512,2048]{1,0:T(8,128)S(1)}, u32[]{:S(2)}) copy-start(f32[512,2048]{1,0:T(8,128)S(1)} %get-tuple-element.81) | copy-start | bytes 12582916
  163.8 14.3 %copy-start.14 = (f32[512,2048]{1,0:T(8,128)}, f32[512,2048]{1,0:T(8,128)S(1)}, u32[]{:S(2)}) copy-start(f32[512,2048]{1,0:T(8,128)S(1)} %get-tuple-element.83) | copy-start | bytes 12582916
  165.2 13.8 copy-start.4
  166.6 13.4 copy-start.8
  167.9 12.9 copy-start.12
  169.5 12.3 copy-start.16
  209.8 19.0 %copy-start.46 = (bf16[2,512,512]{2,1,0:T(8,128)(2,1)S(1)}, bf16[2,512,512]{2,1,0:T(8,128)(2,1)}, u32[]{:S(2)}) copy-start(bf16[2,512,512]{2,1,0:T(8,128)(2,1)} %param.14) | copy-start | bytes 3145732
  209.8 136.9 %all-gather.27.cloned.1.call-start = ((), (), s32[]{:S(2)}) async-start(), calls=%async_computation.29 | async-start | bytes 5242880 | tf_op jit(solution)/shard_map/all_gather | solution.py:46
  228.5 173.5 %all-gather.29.cloned.1.call-start = ((), (), s32[]{:S(2)}) async-start(), calls=%async_computation.31 | async-start | bytes 9437184 | tf_op jit(solution)/shard_map/all_gather | solution.py:46
  258.7 225.6 %all-gather.25.cloned.1.call-start = ((), (), s32[]{:S(2)}) async-start(), calls=%async_computation.28 | async-start | bytes 5242880 | tf_op jit(solution)/shard_map/all_gather | solution.py:46
  278.8 260.5 %all-gather.23.cloned.1.call-start = ((), (), s32[]{:S(2)}) async-start(), calls=%async_computation.27 | async-start | bytes 9437184 | tf_op jit(solution)/shard_map/all_gather | solution.py:46
  284.7 361.2 %reduce-scatter.15.cloned.1.call-start = ((), (), s32[]{:S(2)}) async-start(), calls=%async_computation.32 | async-start | bytes 9437184 | tf_op jit(solution)/shard_map/reduce_scatter | solution.py:50
  539.3 24.1 %copy-start.59 = (bf16[1024,2048]{0,1:T(8,128)(2,1)S(1)}, bf16[1024,2048]{0,1:T(8,128)(2,1)}, u32[]{:S(2)}) copy-start(bf16[1024,2048]{0,1:T(8,128)(2,1)} %all-gather.25.cloned.1.call-done) | copy-start | bytes 12582916
  574.4 146.1 %reduce-scatter.13.cloned.1.call-start = ((), (), s32[]{:S(2)}) async-start(), calls=%async_computation.30 | async-start | bytes 9437184 | tf_op jit(solution)/shard_map/reduce_scatter | solution.py:50
  589.9 56.0 %copy-start.37 = (bf16[256,2048]{1,0:T(8,128)(2,1)S(1)}, bf16[256,2048]{1,0:T(8,128)(2,1)}, u32[]{:S(2)}) copy-start(bf16[256,2048]{1,0:T(8,128)(2,1)} %reduce-scatter.11.cloned.1.call-done) | copy-start | bytes 3145732
  589.9 130.6 %copy-start.38 = (bf16[4,32,8,512]{3,2,0,1:T(8,128)(2,1)S(1)}, bf16[4,32,8,512]{3,2,0,1:T(8,128)(2,1)}, u32[]{:S(2)}) copy-start(bf16[4,32,8,512]{3,2,0,1:T(8,128)(2,1)} %copy.71) | copy-start | bytes 3145732
  589.9 170.5 %all-gather.31.cloned.1.call-start = ((), (), s32[]{:S(2)}) async-start(), calls=%async_computation.33 | async-start | bytes 5242880 | tf_op jit(solution)/shard_map/all_gather | solution.py:46
  725.8 158.1 %reduce-scatter.29.cloned.1.call-start = ((), (), s32[]{:S(2)}) async-start(), calls=%async_computation.42 | async-start | bytes 5242880 | tf_op jit(solution)/shard_map/reduce_scatter | solution.py:50
  742.0 23.7 %copy-start.20 = (bf16[4,2,512,256]{3,2,0,1:T(8,128)(2,1)S(1)}, bf16[4,2,512,256]{3,2,0,1:T(8,128)(2,1)}, u32[]{:S(2)}) copy-start(bf16[4,2,512,256]{3,2,0,1:T(8,128)(2,1)} %copy-done.19) | copy-start | bytes 6291460
  742.0 170.9 %reduce-scatter.19.cloned.1.call-start = ((), (), s32[]{:S(2)}) async-start(), calls=%async_computation.35 | async-start | bytes 2228224 | tf_op jit(solution)/shard_map/reduce_scatter | solution.py:50
  765.7 9.6 copy-start.40
  778.5 6.8 copy-start.24
  813.3 7.4 copy-start.32
  820.8 8.3 copy-start.41
  850.8 140.2 %reduce-scatter.27.cloned.1.call-start = ((), (), s32[]{:S(2)}) async-start(), calls=%async_computation.40 | async-start | bytes 5242880 | tf_op jit(solution)/shard_map/reduce_scatter | solution.py:50
  864.9 172.6 %reduce-scatter.21.cloned.1.call-start = ((), (), s32[]{:S(2)}) async-start(), calls=%async_computation.36 | async-start | bytes 2621440 | tf_op jit(solution)/shard_map/reduce_scatter | solution.py:50
  866.6 6.1 copy-start.25
  883.8 20.6 %copy-start.47 = (bf16[2,512,512]{2,1,0:T(8,128)(2,1)S(1)}, bf16[2,512,512]{2,1,0:T(8,128)(2,1)}, u32[]{:S(2)}) copy-start(bf16[2,512,512]{2,1,0:T(8,128)(2,1)} %copy.57) | copy-start | bytes 3145732
  883.8 187.6 %all-gather.35.cloned.1.call-start = ((), (), s32[]{:S(2)}) async-start(), calls=%async_computation.43 | async-start | bytes 3145728 | tf_op jit(solution)/shard_map/all_gather | solution.py:46
  904.3 213.4 %reduce-scatter.25.cloned.1.call-start = ((), (), s32[]{:S(2)}) async-start(), calls=%async_computation.39 | async-start | bytes 2621440 | tf_op jit(solution)/shard_map/reduce_scatter | solution.py:50
  910.3 234.7 %reduce-scatter.23.cloned.1.call-start = ((), (), s32[]{:S(2)}) async-start(), calls=%async_computation.37 | async-start | bytes 1310720 | tf_op jit(solution)/shard_map/reduce_scatter | solution.py:50
  915.7 283.5 %reduce-scatter.17.cloned.1.call-start = ((), (), s32[]{:S(2)}) async-start(), calls=%async_computation.34 | async-start | bytes 5242880 | tf_op jit(solution)/shard_map/reduce_scatter | solution.py:50
  921.7 312.7 %all-gather.33.cloned.1.call-start = ((), (), s32[]{:S(2)}) async-start(), calls=%async_computation.41 | async-start | bytes 3145728 | tf_op jit(solution)/shard_map/all_gather | solution.py:46
  1039.5 105.5 %all-to-all-start.7 = ((bf16[4,128,512]{2,1,0:T(8,128)(2,1)}), bf16[4,128,512]{2,1,0:T(8,128)(2,1)S(1)}, u32[]{:S(2)}, u32[]{:S(2)}) async-start(bf16[4,128,512]{2,1,0:T(8,128)(2,1)} %pad_maximum_fusion.6), calls=%async_computation.13 | async-start | bytes 1048576 | tf_op jit(solution)/shard_map/all_to_all | solution.py:40
  1043.0 265.4 %all-reduce.4.cloned.1.call-start = ((), (), s32[]{:S(2)}) async-start(), calls=%async_computation.38 | async-start | bytes 524288 | tf_op jit(solution)/shard_map/psum | solution.py:188
  1044.5 104.0 %copy-start.43 = (bf16[256,2048]{1,0:T(8,128)(2,1)S(1)}, bf16[256,2048]{1,0:T(8,128)(2,1)}, u32[]{:S(2)}) copy-start(bf16[256,2048]{1,0:T(8,128)(2,1)} %get-tuple-element.27) | copy-start | bytes 3145732
  1145.0 12.3 all-to-all-start.8
  1148.5 50.6 %copy-start.49 = (bf16[256,256]{1,0:T(8,128)(2,1)S(1)}, bf16[256,256]{1,0:T(8,128)(2,1)}, u32[]{:S(2)}) copy-start(bf16[256,256]{1,0:T(8,128)(2,1)} %reduce-scatter.19.cloned.1.call-done) | copy-start | bytes 393220
  1148.5 50.6 %copy-start.51 = (f32[1,2048]{1,0:T(1,128)S(1)}, f32[1,2048]{1,0:T(1,128)}, u32[]{:S(2)}) copy-start(f32[1,2048]{1,0:T(1,128)} %copy-done.50) | copy-start | bytes 24580
  1157.3 48.2 %all-to-all-start.4 = ((bf16[4,256,512]{2,1,0:T(8,128)(2,1)}), bf16[4,256,512]{2,1,0:T(8,128)(2,1)S(1)}, u32[]{:S(2)}, u32[]{:S(2)}) async-start(bf16[4,256,512]{2,1,0:T(8,128)(2,1)} %pad_maximum_fusion.1), calls=%async_computation.6 | async-start | bytes 2097152 | tf_op jit(solution)/shard_map/all_to_all | solution.py:40
  1160.9 190.0 %all-reduce.6.cloned.1.call-start = ((), (), s32[]{:S(2)}) async-start(), calls=%async_computation.44 | async-start | bytes 2097152 | tf_op jit(solution)/shard_map/psum | solution.py:191
  1160.9 41.3 %copy-start.39 = (f32[256,2048]{1,0:T(8,128)S(1)}, f32[256,2048]{1,0:T(8,128)}, u32[]{:S(2)}) copy-start(f32[256,2048]{1,0:T(8,128)} %get-tuple-element.26) | copy-start | bytes 6291460
  1205.5 189.8 %all-to-all-start.6 = ((bf16[4,256,512]{2,1,0:T(8,128)(2,1)}), bf16[4,256,512]{2,1,0:T(8,128)(2,1)}, u32[]{:S(2)}, u32[]{:S(2)}) async-start(bf16[4,256,512]{2,1,0:T(8,128)(2,1)} %pad_maximum_fusion.3), calls=%async_computation.11 | async-start | bytes 2097152 | tf_op jit(solution)/shard_map/all_to_all | solution.py:40
  1234.4 164.2 %copy-start.1 = (bf16[2048,512]{1,0:T(8,128)(2,1)S(1)}, bf16[2048,512]{1,0:T(8,128)(2,1)}, u32[]{:S(2)}) copy-start(bf16[2048,512]{1,0:T(8,128)(2,1)} %param.23) | copy-start | bytes 6291460
  (26 other events, 87.3 us)
Sparse Core Ops, SparseCore 0:
  9.6 37.4 all-gather.12
  48.7 17.0 all-gather.16
  67.9 46.2 all-gather.14
  116.8 39.6 all-gather.18
  158.4 44.9 all-gather.20
  209.9 53.9 reduce-scatter.10
  266.2 80.5 all-gather.26
  349.4 52.5 all-gather.28
  403.6 80.5 all-gather.24
  486.7 52.5 all-gather.22
  574.6 71.3 reduce-scatter.14
  649.2 71.2 reduce-scatter.12
  725.9 34.4 all-gather.30
  762.7 76.7 reduce-scatter.28
  850.9 61.9 reduce-scatter.18
  915.2 75.7 reduce-scatter.26
  993.1 44.3 reduce-scatter.20
  1039.0 32.4 all-gather.34
  1073.9 43.8 reduce-scatter.24
  1120.7 24.2 reduce-scatter.22
  1148.3 50.8 reduce-scatter.16
  1201.3 33.0 all-gather.32
  1237.8 70.5 all-reduce.3
  1311.3 39.5 all-reduce.5
